TPU v7x, 32 devices: a whole 2x2x4 slice. The times are simulated.
32 devices in a mesh: col: 2 (over x), row: 16 (over z, y, core).
Axes of the slice: x: 2, y: 2, z: 4, core: 2. Of those that a mesh axis runs over, the one named last changes fastest.
Arguments:
- residual: bfloat16 [1024, 2880], P('row'), may hold values from -6 to 6
- query_states: bfloat16 [1024, 4096], P('row', 'col'), may hold values from -48 to 48
- key_states: bfloat16 [1024, 512], P('row'), may hold values from -24 to 24
- value_states: bfloat16 [1024, 512], P('row'), may hold values from -6 to 6
- segment_ids: int32 [1024], P('row'), may hold values from 0 to 3, never falling along the last dimension, each value on 1 to 512 neighbouring positions
- sink_logits: float32 [64], P('col'), may hold values from -2 to 4
- w_out: bfloat16 [4096, 2880], P('col'), may hold values from -0.375 to 0.375
- norm_gain: float32 [2880], replicated, may hold values from 0.5 to 1.5
- expert_ids: int32 [1024, 4], P('row'), may hold values from 0 to 15, all different within a row; in each aligned block of 64 rows (0 to 63, 64 to 127, ...) at most 32 rows name the same one
- route_weight: float32 [1024, 4], P('row'), may hold values from 0.05 to 0.45
- w_gate_up: bfloat16 [16, 2, 2880, 2880], P('row', None, None, 'col'), may hold values from -0.109375 to 0.109375
- w_down: bfloat16 [16, 2880, 2880], P('row', 'col'), may hold values from -0.109375 to 0.109375
Outputs:
- layer_out: bfloat16 [1024, 2880], P('row', 'col')
Inputs may be any that keep to these rules, and one draw needn't show every extreme that they name: `expert_ids`: each token names 4 different experts; among the 64 tokens of one index of row no expert is named by more than 32 tokens, and in every draw some expert is named by exactly 32 of them. `segment_ids`: segment numbers never fall along the tokens.
All inputs are finite; a program needn't handle non-finite values.
Results may differ from a plain program's by a relative error of at most 0.018.
Values may be sent and summed in bfloat16 or wider, within the bound.
A program may use at most 128 MiB of HBM per device.

v0:
```python
import jax
import jax.numpy as jnp
from jax import lax
from jax.sharding import PartitionSpec as P

HEADS = 64
KV_HEADS = 8
HEAD_DIM = 64
WINDOW = 128
TOP = 4
epsilon = 1e-05
masked_score = -1e30


def shifted(shard, axis, by):
    size = lax.axis_size(axis)
    pairs = [(i, i + by) for i in range(size) if 0 <= i + by < size]
    return lax.ppermute(shard, axis, pairs)


def normalize(stream_rows, norm_gain):
    values32 = stream_rows.astype(jnp.float32)
    square_mean = jnp.mean(values32 * values32, axis=-1, keepdims=True)
    return (values32 * lax.rsqrt(square_mean + epsilon) * norm_gain).astype(jnp.bfloat16)


def attend(query_groups, key_groups, value_groups, allowed, sink_groups):
    scores = jnp.einsum(
        "tgjd,lgd->gjtl", query_groups, key_groups, preferred_element_type=jnp.float32
    )
    scores = scores * query_groups.shape[-1] ** (-0.5)
    scores = jnp.where(allowed[None, None], scores, masked_score)
    peak_score = jnp.maximum(jnp.max(scores, axis=-1, keepdims=True), sink_groups)
    numerator = jnp.exp(scores - peak_score)
    denominator = jnp.exp(sink_groups - peak_score) + jnp.sum(numerator, axis=-1, keepdims=True)
    weights = (numerator / denominator).astype(jnp.bfloat16)
    return jnp.einsum(
        "gjtl,lgd->tgjd", weights, value_groups, preferred_element_type=jnp.float32
    ).astype(jnp.bfloat16)


def local(
    residual,
    query_states,
    key_states,
    value_states,
    segment_ids,
    sink_logits,
    w_out,
    norm_gain,
    expert_ids,
    route_weight,
    w_gate_up,
    w_down,
):
    tok_rows = query_states.shape[0]
    row_count = lax.axis_size("row")
    col_count = lax.axis_size("col")
    row_index = lax.axis_index("row")
    col_index = lax.axis_index("col")
    local_heads = sink_logits.shape[0]
    group_size = HEADS // KV_HEADS
    if local_heads >= group_size:
        kv_count = local_heads // group_size
        kv_first = col_index * kv_count
    else:
        kv_count = 1
        kv_first = col_index * local_heads // group_size
    kv_width = kv_count * HEAD_DIM
    own_keys = lax.dynamic_slice_in_dim(key_states, kv_first * HEAD_DIM, kv_width, 1)
    own_values = lax.dynamic_slice_in_dim(value_states, kv_first * HEAD_DIM, kv_width, 1)
    shift_count = (WINDOW + tok_rows - 2) // tok_rows
    key_parts = []
    value_parts = []
    segment_parts = []
    start_parts = []
    for offset in range(shift_count, 0, -1):
        arrived = shifted((own_keys, own_values, segment_ids), "row", offset)
        key_parts.append(arrived[0])
        value_parts.append(arrived[1])
        segment_parts.append(arrived[2])
        start_parts.append((row_index - offset) * tok_rows)
    key_parts.append(own_keys)
    value_parts.append(own_values)
    segment_parts.append(segment_ids)
    start_parts.append(row_index * tok_rows)
    key_groups = jnp.concatenate(key_parts, 0).reshape(-1, kv_count, HEAD_DIM)
    value_groups = jnp.concatenate(value_parts, 0).reshape(-1, kv_count, HEAD_DIM)
    key_segments = jnp.concatenate(segment_parts, 0)
    positions = jnp.arange(tok_rows, dtype=jnp.int32)
    key_position = jnp.concatenate([start + positions for start in start_parts], 0)
    query_position = row_index * tok_rows + positions
    allowed = (key_position[None, :] >= 0) & (key_position[None, :] <= query_position[:, None])
    allowed = allowed & (key_position[None, :] > query_position[:, None] - WINDOW)
    allowed = allowed & (key_segments[None, :] == segment_ids[:, None])
    query_groups = query_states.reshape(tok_rows, kv_count, local_heads // kv_count, HEAD_DIM)
    sink_groups = sink_logits.reshape(kv_count, local_heads // kv_count, 1, 1)
    attended = attend(query_groups, key_groups, value_groups, allowed, sink_groups).reshape(
        tok_rows, local_heads * HEAD_DIM
    )
    partial_value = jnp.dot(attended, w_out, preferred_element_type=jnp.float32)
    feature_count = residual.shape[1] // col_count
    experts_all = w_gate_up.shape[0] * row_count
    slot_cap = max(2, 2 * TOP * tok_rows // experts_all)
    routing = jnp.concatenate([expert_ids.astype(jnp.float32), route_weight], 1)
    routing = lax.all_gather(routing, "row", axis=0, tiled=False)
    names_mine = routing[:, :, :TOP] == row_index.astype(jnp.float32)
    mine = jnp.any(names_mine, axis=2)
    weight = jnp.sum(jnp.where(names_mine, routing[:, :, TOP:], 0.0), axis=2)
    slot_of = jnp.cumsum(mine.astype(jnp.int32), axis=1) - 1
    slots = jnp.arange(slot_cap, dtype=jnp.int32)
    chosen = mine[:, None, :] & (slot_of[:, None, :] == slots[None, :, None])
    selector = chosen.astype(jnp.bfloat16)
    combine = jnp.where(chosen, weight[:, None, :], 0.0)
    expert_gate_up = w_gate_up[0]
    expert_down = w_down[0]
    summed = lax.psum(partial_value.astype(jnp.bfloat16), "col").astype(jnp.float32)
    stream = (residual.astype(jnp.float32) + summed).astype(jnp.bfloat16)
    stream_part = lax.dynamic_slice_in_dim(stream, col_index * feature_count, feature_count, 1)
    source_rows = normalize(stream, norm_gain)
    gathered = lax.all_gather(source_rows, "row", axis=0, tiled=False)
    packed = (
        jnp.einsum("nst,ntd->nsd", selector, gathered, preferred_element_type=jnp.float32)
        .astype(jnp.bfloat16)
        .reshape(row_count * slot_cap, -1)
    )
    gate = jnp.dot(packed, expert_gate_up[0], preferred_element_type=jnp.float32)
    up = jnp.dot(packed, expert_gate_up[1], preferred_element_type=jnp.float32)
    active = ((up + 1.0) * gate * jax.nn.sigmoid(1.702 * gate)).astype(jnp.bfloat16)
    expert_partial = jnp.dot(active, expert_down, preferred_element_type=jnp.float32)
    scaled = expert_partial.reshape(row_count, slot_cap, -1) * jnp.sum(combine, 2)[:, :, None]
    mixed = (
        jnp.einsum(
            "nst,nsd->ntd",
            selector,
            scaled.astype(jnp.bfloat16),
            preferred_element_type=jnp.float32,
        )
        .astype(jnp.bfloat16)
        .reshape(row_count * tok_rows, -1)
    )
    mixed = lax.psum_scatter(mixed, "row", scatter_dimension=0, tiled=True)
    mixed = lax.psum_scatter(mixed, "col", scatter_dimension=1, tiled=True)
    return (stream_part.astype(jnp.float32) + mixed.astype(jnp.float32)).astype(jnp.bfloat16)


def solution(mesh):
    in_specs = (
        P("row", None),
        P("row", "col"),
        P("row", None),
        P("row", None),
        P("row"),
        P("col"),
        P("col", None),
        P(),
        P("row", None),
        P("row", None),
        P("row", None, None, "col"),
        P("row", "col", None),
    )
    out_specs = P("row", "col")
    return jax.shard_map(local, mesh=mesh, in_specs=in_specs, out_specs=out_specs, check_vma=False)
```

profile of v0, /device:TPU:0, one launch (start us, length us, event | category | flops | bytes accessed | tf_op | source)
XLA Modules:
  0.0 268.6 jit_solution(8531859856784551742)
XLA Ops:
  6.5 0.0 copy-start
  6.5 0.0 all-reduce.2.cloned.1.call-start
  6.5 2.5 collective-permute-start.3
  9.1 4.4 %collective-permute-start.2 = (s32[64]{0:T(128)}, s32[64]{0:T(128)S(1)}, u32[]{:S(2)}, u32[]{:S(2)}) collective-permute-start(s32[64]{0:T(128)} %param.16), channel_id=1, source_target_pairs={{0,2},{1,3},{2,4},{3,5},{4,6},{5,7},{6,8},{7,9},{8,10},{9,11},{10,... | collective-permute-start | bytes 776 | tf_op jit(solution)/shard_map/ppermute | solution.py:18
  13.5 0.0 copy-done
  13.5 3.2 %collective-permute-start.1 = (bf16[64,256]{1,0:T(8,128)(2,1)S(1)}, bf16[64,256]{1,0:T(8,128)(2,1)S(1)}, u32[]{:S(2)}, u32[]{:S(2)}) collective-permute-start(bf16[64,256]{1,0:T(8,128)(2,1)S(1)} %constant_dynamic-slice_fusion.1), channel_id=1, source_target_pairs={{0,1},{1,2},{2,3},{3,4},{4,5},{5,6},{6,7},{7,8},{8,9},{9,10},{10,1... | collective-permute-start | bytes 98312 | tf_op jit(solution)/shard_map/ppermute | solution.py:18
  16.8 3.4 %collective-permute-start = (bf16[64,256]{1,0:T(8,128)(2,1)S(1)}, bf16[64,256]{1,0:T(8,128)(2,1)S(1)}, u32[]{:S(2)}, u32[]{:S(2)}) collective-permute-start(bf16[64,256]{1,0:T(8,128)(2,1)S(1)} %constant_dynamic-slice_fusion.1), channel_id=1, source_target_pairs={{0,2},{1,3},{2,4},{3,5},{4,6},{5,7},{6,8},{7,9},{8,10},{9,11},{10,... | collective-permute-start | bytes 98312 | tf_op jit(solution)/shard_map/ppermute | solution.py:18
  20.2 0.8 constant_dynamic-slice_fusion
  21.0 1.9 collective-permute-start.5
  22.9 0.1 broadcast_compare_fusion
  23.0 0.7 max.18
  23.8 1.5 reshape.191
  25.2 0.0 collective-permute-done.3
  25.2 3.4 %collective-permute-start.4 = (bf16[64,256]{1,0:T(8,128)(2,1)S(1)}, bf16[64,256]{1,0:T(8,128)(2,1)S(1)}, u32[]{:S(2)}, u32[]{:S(2)}) collective-permute-start(bf16[64,256]{1,0:T(8,128)(2,1)S(1)} %constant_dynamic-slice_fusion), channel_id=1, source_target_pairs={{0,2},{1,3},{2,4},{3,5},{4,6},{5,7},{6,8},{7,9},{8,10},{9,11},{10,... | collective-permute-start | bytes 98312 | tf_op jit(solution)/shard_map/ppermute | solution.py:18
  28.7 0.0 collective-permute-done.2
  28.7 0.7 pad_add_fusion.1
  29.4 0.7 compare_and_fusion
  30.2 0.0 collective-permute-done.1
  30.2 0.0 collective-permute-done
  30.2 0.1 copy.20
  30.3 0.0 collective-permute-done.5
  30.3 0.0 collective-permute-done.4
  30.4 0.1 copy.21
  30.5 0.0 copy-start.1
  30.5 0.6 fusion.37
  31.0 0.1 broadcast_maximum_fusion
  31.1 0.7 fusion.22
  31.8 0.1 exponential_add_fusion
  31.9 1.1 convolution_convert_fusion.3
  33.0 1.9 copy-done.1
  34.8 0.0 copy-start.2
  34.8 0.0 copy-start.3
  34.8 0.0 copy-start.4
  34.8 0.0 copy-start.5
  34.8 4.4 %convolution_convert_fusion.2 = bf16[64,2880]{1,0:T(8,128)(2,1)} fusion(bf16[64,2048]{0,1:T(8,128)(2,1)S(1)} %bitcast.59, bf16[2048,2880]{0,1:T(8,128)(2,1)S(1)} %copy-done.1), kind=kOutput, calls=%fused_computation.11 | convolution fusion | flops 755159040 | bytes 12427264 | tf_op jit(solution)/shard_map/dot_general | solution.py:101
  39.3 0.0 all-reduce.2.cloned.1.call-update
  39.3 0.0 all-gather.5.cloned.1.call-start
  39.3 26.4 %all-reduce.2.cloned.1.call-done = bf16[64,2880]{1,0:T(8,128)(2,1)} async-done(((bf16[64,2880]{1,0:T(8,128)(2,1)}), bf16[64,2880]{1,0:T(8,128)(2,1)}) %all-reduce.2.cloned.1.call-update) | async-done | bytes 368656 | tf_op jit(solution)/shard_map/psum | solution.py:117
  65.7 0.0 copy-done.2
  65.7 1.2 fusion.23
  67.0 0.0 copy-done.3
  67.0 0.9 fusion.25
  67.9 0.0 all-gather.5.cloned.1.call-update
  67.9 0.0 reduce-scatter.5.cloned.1.call-start
  68.0 0.0 copy-done.4
  68.0 0.0 copy-done.5
  68.0 22.1 %all-gather.2 = f32[16,64,8]{1,2,0:T(8,128)S(1)} all-gather(f32[1,64,8]{1,2,0:T(8,128)S(1)} %maximum_bitcast_fusion), channel_id=2, replica_groups=mesh['col'=2,'row'=16] {'row'}, dimensions={0}, use_global_device_ids=true | all-gather | bytes 34816 | tf_op jit(solution)/shard_map/all_gather | solution.py:106
  90.2 0.2 reduce_window_sum.11
  90.5 0.1 select_reduce_fusion
  90.6 37.7 %all-gather.5.cloned.1.call-done = bf16[1024,2880]{1,0:T(8,128)(2,1)} async-done(((bf16[64,2880]{1,0:T(8,128)(2,1)}), bf16[1024,2880]{1,0:T(8,128)(2,1)}) %all-gather.5.cloned.1.call-update) | async-done | bytes 5898256 | tf_op jit(solution)/shard_map/all_gather | solution.py:121
  128.4 3.7 %convolution_convert_fusion.1 = bf16[16,32,2880]{2,1,0:T(8,128)(2,1)S(1)} fusion(bf16[16,64,2880]{2,1,0:T(8,128)(2,1)} %bitcast.54, s32[16,64]{1,0:T(8,128)S(1)} %broadcast_add_fusion, pred[16,64]{1,0:T(8,128)(4,1)S(1)} %reduce_or.9), kind=kOutput, calls=%fused_computation.10 | convolution fusion | flops 190283776 | bytes 8852480 | tf_op jit(solution)/shard_map/nst,ntd->nsd/dot_general | solution.py:123
  132.0 7.2 %fusion.2 = f32[512,1440]{0,1:T(8,128)S(1)} fusion(bf16[512,2880]{1,0:T(8,128)(2,1)S(1)} %bitcast.55, bf16[1,2,2880,1440]{2,3,1,0:T(8,128)(2,1)} %param.22), kind=kOutput, calls=%fused_computation.2 | convolution fusion | flops 4246732800 | bytes 14376960 | tf_op jit(solution)/shard_map/dot_general | solution.py:127
  139.2 8.8 %fusion.19 = bf16[512,1440]{0,1:T(8,128)(2,1)S(1)} fusion(f32[512,1440]{0,1:T(8,128)S(1)} %fusion.2, bf16[512,2880]{1,0:T(8,128)(2,1)S(1)} %bitcast.56, bf16[1,2,2880,1440]{2,3,1,0:T(8,128)(2,1)} %param.22), kind=kOutput, calls=%fused_computation.15 | convolution fusion | flops 4252631040 | bytes 15851520 | tf_op jit(solution)/shard_map/dot_general | solution.py:128
  148.1 0.7 copy.23
  148.8 10.8 %convolution_convert_fusion = bf16[16,64,2880]{2,1,0:T(8,128)(2,1)} fusion(bf16[16,32,1440]{2,1,0:T(8,128)(2,1)S(1)} %bitcast.58, bf16[1,1440,2880]{2,1,0:T(8,128)(2,1)} %param.23, f32[16,32]{1,0:T(8,128)S(1)} %select_reduce_fusion, s32[16,64]{1,0:T(8,128)S(1)} %broadcast_add_fusion, pred[16,64]{1,0:T(8,128)(4,1)S(1)} %reduce_or.9), kind=kOutput, calls=%fused_computation.9 | convolution fusion | flops 4441440256 | bytes 15674368 | tf_op jit(solution)/shard_map/nst,nsd->ntd/dot_general | solution.py:133
  159.6 0.0 reduce-scatter.5.cloned.1.call-update
  159.6 0.0 reduce-scatter.7.cloned.1.call-start
  159.6 82.0 %reduce-scatter.5.cloned.1.call-done = bf16[64,2880]{1,0:T(8,128)(2,1)} async-done(((bf16[1024,2880]{1,0:T(8,128)(2,1)}), bf16[64,2880]{1,0:T(8,128)(2,1)}) %reduce-scatter.5.cloned.1.call-update) | async-done | bytes 368656 | tf_op jit(solution)/shard_map/reduce_scatter | solution.py:142
  241.6 2.1 copy.26
  243.7 0.0 reduce-scatter.7.cloned.1.call-update
  243.8 16.3 %reduce-scatter.7.cloned.1.call-done = bf16[1440,64]{1,0:T(8,128)(2,1)} async-done(((bf16[2880,64]{1,0:T(8,128)(2,1)}), bf16[1440,64]{1,0:T(8,128)(2,1)}) %reduce-scatter.7.cloned.1.call-update) | async-done | bytes 184336
  260.1 1.1 copy.27
  261.2 0.8 add_convert_fusion.1
  (12 shorter events, 0.1 us)
Async XLA Ops:
  6.5 7.0 %copy-start = (bf16[64,512]{1,0:T(8,128)(2,1)S(1)}, bf16[64,512]{1,0:T(8,128)(2,1)}, u32[]{:S(2)}) copy-start(bf16[64,512]{1,0:T(8,128)(2,1)} %param.15) | copy-start | bytes 196612
  6.5 59.2 %all-reduce.2.cloned.1.call-start = ((), (), s32[]{:S(2)}) async-start(), calls=%async_computation.2 | async-start | bytes 753664 | tf_op jit(solution)/shard_map/psum | solution.py:117
  6.5 18.7 %collective-permute-start.3 = (s32[64]{0:T(128)}, s32[64]{0:T(128)S(1)}, u32[]{:S(2)}, u32[]{:S(2)}) collective-permute-start(s32[64]{0:T(128)} %param.16), channel_id=1, source_target_pairs={{0,1},{1,2},{2,3},{3,4},{4,5},{5,6},{6,7},{7,8},{8,9},{9,10},{10,1... | collective-permute-start | bytes 776 | tf_op jit(solution)/shard_map/ppermute | solution.py:18
  9.1 19.6 %collective-permute-start.2 = (s32[64]{0:T(128)}, s32[64]{0:T(128)S(1)}, u32[]{:S(2)}, u32[]{:S(2)}) collective-permute-start(s32[64]{0:T(128)} %param.16), channel_id=1, source_target_pairs={{0,2},{1,3},{2,4},{3,5},{4,6},{5,7},{6,8},{7,9},{8,10},{9,11},{10,... | collective-permute-start | bytes 776 | tf_op jit(solution)/shard_map/ppermute | solution.py:18
  13.5 16.6 %collective-permute-start.1 = (bf16[64,256]{1,0:T(8,128)(2,1)S(1)}, bf16[64,256]{1,0:T(8,128)(2,1)S(1)}, u32[]{:S(2)}, u32[]{:S(2)}) collective-permute-start(bf16[64,256]{1,0:T(8,128)(2,1)S(1)} %constant_dynamic-slice_fusion.1), channel_id=1, source_target_pairs={{0,1},{1,2},{2,3},{3,4},{4,5},{5,6},{6,7},{7,8},{8,9},{9,10},{10,1... | collective-permute-start | bytes 98312 | tf_op jit(solution)/shard_map/ppermute | solution.py:18
  16.8 13.4 %collective-permute-start = (bf16[64,256]{1,0:T(8,128)(2,1)S(1)}, bf16[64,256]{1,0:T(8,128)(2,1)S(1)}, u32[]{:S(2)}, u32[]{:S(2)}) collective-permute-start(bf16[64,256]{1,0:T(8,128)(2,1)S(1)} %constant_dynamic-slice_fusion.1), channel_id=1, source_target_pairs={{0,2},{1,3},{2,4},{3,5},{4,6},{5,7},{6,8},{7,9},{8,10},{9,11},{10,... | collective-permute-start | bytes 98312 | tf_op jit(solution)/shard_map/ppermute | solution.py:18
  21.0 9.3 %collective-permute-start.5 = (bf16[64,256]{1,0:T(8,128)(2,1)S(1)}, bf16[64,256]{1,0:T(8,128)(2,1)S(1)}, u32[]{:S(2)}, u32[]{:S(2)}) collective-permute-start(bf16[64,256]{1,0:T(8,128)(2,1)S(1)} %constant_dynamic-slice_fusion), channel_id=1, source_target_pairs={{0,1},{1,2},{2,3},{3,4},{4,5},{5,6},{6,7},{7,8},{8,9},{9,10},{10,1... | collective-permute-start | bytes 98312 | tf_op jit(solution)/shard_map/ppermute | solution.py:18
  25.2 5.1 %collective-permute-start.4 = (bf16[64,256]{1,0:T(8,128)(2,1)S(1)}, bf16[64,256]{1,0:T(8,128)(2,1)S(1)}, u32[]{:S(2)}, u32[]{:S(2)}) collective-permute-start(bf16[64,256]{1,0:T(8,128)(2,1)S(1)} %constant_dynamic-slice_fusion), channel_id=1, source_target_pairs={{0,2},{1,3},{2,4},{3,5},{4,6},{5,7},{6,8},{7,9},{8,10},{9,11},{10,... | collective-permute-start | bytes 98312 | tf_op jit(solution)/shard_map/ppermute | solution.py:18
  30.5 4.4 %copy-start.1 = (bf16[2048,2880]{0,1:T(8,128)(2,1)S(1)}, bf16[2048,2880]{0,1:T(8,128)(2,1)}, u32[]{:S(2)}) copy-start(bf16[2048,2880]{0,1:T(8,128)(2,1)} %param.18) | copy-start | bytes 35389444
  34.8 30.9 %copy-start.2 = (bf16[64,2880]{1,0:T(8,128)(2,1)S(1)}, bf16[64,2880]{1,0:T(8,128)(2,1)}, u32[]{:S(2)}) copy-start(bf16[64,2880]{1,0:T(8,128)(2,1)} %param.12) | copy-start | bytes 1105924
  34.8 32.2 %copy-start.3 = (f32[2880]{0:T(1024)S(1)}, f32[2880]{0:T(1024)}, u32[]{:S(2)}) copy-start(f32[2880]{0:T(1024)} %param.19) | copy-start | bytes 34564
  34.8 33.2 %copy-start.4 = (s32[64,4]{0,1:T(4,128)S(1)}, s32[64,4]{0,1:T(4,128)}, u32[]{:S(2)}) copy-start(s32[64,4]{0,1:T(4,128)} %param.20) | copy-start | bytes 3076
  34.8 33.2 %copy-start.5 = (f32[64,4]{0,1:T(4,128)S(1)}, f32[64,4]{0,1:T(4,128)}, u32[]{:S(2)}) copy-start(f32[64,4]{0,1:T(4,128)} %param.21) | copy-start | bytes 3076
  39.3 89.1 %all-gather.5.cloned.1.call-start = ((), (), s32[]{:S(2)}) async-start(), calls=%async_computation.4 | async-start | bytes 6406144 | tf_op jit(solution)/shard_map/all_gather | solution.py:121
  67.9 173.7 %reduce-scatter.5.cloned.1.call-start = ((), (), s32[]{:S(2)}) async-start(), calls=%async_computation.3 | async-start | bytes 6406144 | tf_op jit(solution)/shard_map/reduce_scatter | solution.py:142
  159.6 100.5 %reduce-scatter.7.cloned.1.call-start = ((), (), s32[]{:S(2)}) async-start(), calls=%async_computation.5 | async-start | bytes 1105920
Sparse Core Ops, SparseCore 0:
  39.4 26.2 all-reduce.1
  68.0 60.2 all-gather.4
  159.7 81.8 reduce-scatter.4
  243.9 16.1 reduce-scatter.6
where the time goes:
time: 269 us
  waiting for transfers between devices  163 us (61%)
  matrix products  36.5 us (14%)
  blocking collectives  22.1 us (8%)
  starting transfers between devices  19.1 us (7%)
  between operations  13.4 us (5%)
  local copies, waits for them, and re-layouts  9.04 us (3%)
  other arithmetic  5.84 us (2%)
    reduce_scatter x1, waiting for transfers between devices, local(): mixed = lax.psum_scatter(mixed, 'row', scatter_dimension=0, tiled=True)  82 us
    all_gather x1, waiting for transfers between devices, local(): gathered = lax.all_gather(source_rows, 'row', axis=0, tiled=False)  37.7 us
    psum x1, waiting for transfers between devices, local(): lax.psum(partial_value.astype(jnp.bfloat16), 'col').astype(jnp.float32)  26.4 us
    all_gather x1, blocking collectives, local(): routing = lax.all_gather(routing, 'row', axis=0, tiled=False)  22.1 us
    ppermute x6, starting transfers between devices, shifted(): return lax.ppermute(shard, axis, pairs)  19 us
    unnamed x5, waiting for transfers between devices  16.4 us
    dot_general x1, matrix products, local(): jnp.einsum('nst,nsd->ntd', selector, scaled.astype(jnp.bfloat16), preferr...  10.8 us
    dot_general x1, matrix products, local(): up = jnp.dot(packed, expert_gate_up[1], preferred_element_type=jnp.float32)  8.82 us
  transfers between devices with their start and end apart: 10, of which 4 were waited for; matrix products, arithmetic and copies ran while one was open for 2% of the time, Pallas kernels for 0%

commit v1 on v0

--- a/solution.py
+++ b/solution.py
@@ -114,7 +114,9 @@
     combine = jnp.where(chosen, weight[:, None, :], 0.0)
     expert_gate_up = w_gate_up[0]
     expert_down = w_down[0]
-    summed = lax.psum(partial_value.astype(jnp.bfloat16), "col").astype(jnp.float32)
+    summed = jnp.sum(lax.all_gather(partial_value.astype(jnp.bfloat16), "col"), axis=0).astype(
+        jnp.float32
+    )
     stream = (residual.astype(jnp.float32) + summed).astype(jnp.bfloat16)
     stream_part = lax.dynamic_slice_in_dim(stream, col_index * feature_count, feature_count, 1)
     source_rows = normalize(stream, norm_gain)

time: 269 us -> 253 us (0.941)
  waiting for transfers between devices: 163 us -> 138 us
  blocking collectives: 22.1 us -> 32.3 us
    psum x1 -> x0, waiting for transfers between devices: 26.4 us -> none  [local(): lax.psum(partial_value.astype(jnp.bfloat16), 'col').astype(jnp.float32)]
    all_gather x0 -> x1, blocking collectives: none -> 12.1 us  [local(): lax.all_gather(partial_value.astype(jnp.bfloat16), 'col')]
    unnamed x5 -> x4, waiting for transfers between devices: 16.4 us -> 16.4 us
  transfers between devices with their start and end apart: 10 -> 9, of which waited for: 4 -> 3; matrix products, arithmetic and copies ran while one was open for 2% -> 2% of each run, Pallas kernels for 0% -> 0%
where the time goes in v1:
time: 253 us
  waiting for transfers between devices  138 us (55%)
  matrix products  35.8 us (14%)
  blocking collectives  32.3 us (13%)
  starting transfers between devices  19 us (8%)
  between operations  13.5 us (5%)
  local copies, waits for them, and re-layouts  9.05 us (4%)
  other arithmetic  5.1 us (2%)
    reduce_scatter x1, waiting for transfers between devices, local(): mixed = lax.psum_scatter(mixed, 'row', scatter_dimension=0, tiled=True)  81.9 us
    all_gather x1, waiting for transfers between devices, local(): gathered = lax.all_gather(source_rows, 'row', axis=0, tiled=False)  39.4 us
    all_gather x1, blocking collectives, local(): routing = lax.all_gather(routing, 'row', axis=0, tiled=False)  20.2 us
    ppermute x6, starting transfers between devices, shifted(): return lax.ppermute(shard, axis, pairs)  19 us
    unnamed x4, waiting for transfers between devices  16.4 us
    all_gather x1, blocking collectives, local(): lax.all_gather(partial_value.astype(jnp.bfloat16), 'col')  12.1 us
    dot_general x1, matrix products, local(): jnp.einsum('nst,nsd->ntd', selector, scaled.astype(jnp.bfloat16), preferr...  10.8 us
    dot_general x1, matrix products, local(): up = jnp.dot(packed, expert_gate_up[1], preferred_element_type=jnp.float32)  8.82 us
  transfers between devices with their start and end apart: 9, of which 3 were waited for; matrix products, arithmetic and copies ran while one was open for 2% of the time, Pallas kernels for 0%

profile of v1, /device:TPU:0, one launch (start us, length us, event | category | flops | bytes accessed | tf_op | source)
XLA Modules:
  0.0 252.5 jit_solution(11337429251947719140)
XLA Ops:
  6.5 0.0 copy-start
  6.5 0.0 all-gather.6.cloned.1.call-start
  6.5 2.5 collective-permute-start.3
  9.1 4.4 %collective-permute-start.2 = (s32[64]{0:T(128)}, s32[64]{0:T(128)S(1)}, u32[]{:S(2)}, u32[]{:S(2)}) collective-permute-start(s32[64]{0:T(128)} %param.16), channel_id=1, source_target_pairs={{0,2},{1,3},{2,4},{3,5},{4,6},{5,7},{6,8},{7,9},{8,10},{9,11},{10,... | collective-permute-start | bytes 776 | tf_op jit(solution)/shard_map/ppermute | solution.py:18
  13.5 0.0 copy-done
  13.5 3.2 %collective-permute-start.1 = (bf16[64,256]{1,0:T(8,128)(2,1)S(1)}, bf16[64,256]{1,0:T(8,128)(2,1)S(1)}, u32[]{:S(2)}, u32[]{:S(2)}) collective-permute-start(bf16[64,256]{1,0:T(8,128)(2,1)S(1)} %constant_dynamic-slice_fusion.1), channel_id=1, source_target_pairs={{0,1},{1,2},{2,3},{3,4},{4,5},{5,6},{6,7},{7,8},{8,9},{9,10},{10,1... | collective-permute-start | bytes 98312 | tf_op jit(solution)/shard_map/ppermute | solution.py:18
  16.8 3.4 %collective-permute-start = (bf16[64,256]{1,0:T(8,128)(2,1)S(1)}, bf16[64,256]{1,0:T(8,128)(2,1)S(1)}, u32[]{:S(2)}, u32[]{:S(2)}) collective-permute-start(bf16[64,256]{1,0:T(8,128)(2,1)S(1)} %constant_dynamic-slice_fusion.1), channel_id=1, source_target_pairs={{0,2},{1,3},{2,4},{3,5},{4,6},{5,7},{6,8},{7,9},{8,10},{9,11},{10,... | collective-permute-start | bytes 98312 | tf_op jit(solution)/shard_map/ppermute | solution.py:18
  20.2 0.8 constant_dynamic-slice_fusion
  21.0 1.9 collective-permute-start.5
  22.9 0.1 broadcast_compare_fusion
  23.0 0.7 max.18
  23.8 1.5 reshape.191
  25.2 0.0 collective-permute-done.3
  25.2 3.4 %collective-permute-start.4 = (bf16[64,256]{1,0:T(8,128)(2,1)S(1)}, bf16[64,256]{1,0:T(8,128)(2,1)S(1)}, u32[]{:S(2)}, u32[]{:S(2)}) collective-permute-start(bf16[64,256]{1,0:T(8,128)(2,1)S(1)} %constant_dynamic-slice_fusion), channel_id=1, source_target_pairs={{0,2},{1,3},{2,4},{3,5},{4,6},{5,7},{6,8},{7,9},{8,10},{9,11},{10,... | collective-permute-start | bytes 98312 | tf_op jit(solution)/shard_map/ppermute | solution.py:18
  28.7 0.0 collective-permute-done.2
  28.7 0.7 pad_add_fusion.1
  29.4 0.7 compare_and_fusion
  30.2 0.0 collective-permute-done.1
  30.2 0.0 collective-permute-done
  30.2 0.1 copy.20
  30.3 0.0 collective-permute-done.5
  30.3 0.0 collective-permute-done.4
  30.4 0.1 copy.21
  30.5 0.0 copy-start.2
  30.5 0.6 fusion.37
  31.0 0.1 broadcast_maximum_fusion
  31.1 0.7 fusion.22
  31.8 0.1 exponential_add_fusion
  31.9 1.1 convolution_convert_fusion.3
  33.0 1.9 copy-done.2
  34.8 0.0 copy-start.3
  34.8 3.7 %convolution_convert_fusion.2 = bf16[64,2880]{1,0:T(8,128)(2,1)S(1)} fusion(bf16[64,2048]{0,1:T(8,128)(2,1)S(1)} %bitcast.61, bf16[2048,2880]{0,1:T(8,128)(2,1)S(1)} %copy-done.2), kind=kOutput, calls=%fused_computation.11 | convolution fusion | flops 755159040 | bytes 12427264 | tf_op jit(solution)/shard_map/dot_general | solution.py:101
  38.5 0.0 copy-start.4
  38.5 0.0 copy-start.5
  38.5 0.0 copy-start.6
  38.5 12.1 %all-gather = bf16[128,2880]{1,0:T(8,128)(2,1)S(1)} all-gather(bf16[64,2880]{1,0:T(8,128)(2,1)S(1)} %convolution_convert_fusion.2), channel_id=2, replica_groups=mesh['col'=2,'row'=16] {'col'}, dimensions={0}, use_global_device_ids=true | all-gather | bytes 1105920 | tf_op jit(solution)/shard_map/all_gather | solution.py:117
  50.6 0.3 reduce_sum.49
  50.9 0.0 copy-done.3
  50.9 0.2 fusion.23
  51.1 0.0 copy-done.4
  51.1 0.9 fusion.25
  52.0 0.0 all-gather.6.cloned.1.call-update
  52.1 0.0 reduce-scatter.5.cloned.1.call-start
  52.1 0.0 copy-done.5
  52.1 0.0 copy-done.6
  52.2 20.2 %all-gather.3 = f32[16,64,8]{1,2,0:T(8,128)S(1)} all-gather(f32[1,64,8]{1,2,0:T(8,128)S(1)} %maximum_bitcast_fusion), channel_id=3, replica_groups=mesh['col'=2,'row'=16] {'row'}, dimensions={0}, use_global_device_ids=true | all-gather | bytes 34816 | tf_op jit(solution)/shard_map/all_gather | solution.py:106
  72.5 0.2 reduce_window_sum.11
  72.7 0.1 select_reduce_fusion
  72.9 39.4 %all-gather.6.cloned.1.call-done = bf16[1024,2880]{1,0:T(8,128)(2,1)} async-done(((bf16[64,2880]{1,0:T(8,128)(2,1)}), bf16[1024,2880]{1,0:T(8,128)(2,1)}) %all-gather.6.cloned.1.call-update) | async-done | bytes 5898256 | tf_op jit(solution)/shard_map/all_gather | solution.py:123
  112.3 3.7 %convolution_convert_fusion.1 = bf16[16,32,2880]{2,1,0:T(8,128)(2,1)S(1)} fusion(bf16[16,64,2880]{2,1,0:T(8,128)(2,1)} %bitcast.55, s32[16,64]{1,0:T(8,128)S(1)} %broadcast_add_fusion, pred[16,64]{1,0:T(8,128)(4,1)S(1)} %reduce_or.9), kind=kOutput, calls=%fused_computation.10 | convolution fusion | flops 190283776 | bytes 8852480 | tf_op jit(solution)/shard_map/nst,ntd->nsd/dot_general | solution.py:125
  116.0 7.2 %fusion.2 = f32[512,1440]{0,1:T(8,128)S(1)} fusion(bf16[512,2880]{1,0:T(8,128)(2,1)S(1)} %bitcast.56, bf16[1,2,2880,1440]{2,3,1,0:T(8,128)(2,1)} %param.22), kind=kOutput, calls=%fused_computation.2 | convolution fusion | flops 4246732800 | bytes 14376960 | tf_op jit(solution)/shard_map/dot_general | solution.py:129
  123.2 8.8 %fusion.19 = bf16[512,1440]{0,1:T(8,128)(2,1)S(1)} fusion(f32[512,1440]{0,1:T(8,128)S(1)} %fusion.2, bf16[512,2880]{1,0:T(8,128)(2,1)S(1)} %bitcast.57, bf16[1,2,2880,1440]{2,3,1,0:T(8,128)(2,1)} %param.22), kind=kOutput, calls=%fused_computation.15 | convolution fusion | flops 4252631040 | bytes 15851520 | tf_op jit(solution)/shard_map/dot_general | solution.py:130
  132.0 0.7 copy.23
  132.7 10.8 %convolution_convert_fusion = bf16[16,64,2880]{2,1,0:T(8,128)(2,1)} fusion(bf16[16,32,1440]{2,1,0:T(8,128)(2,1)S(1)} %bitcast.60, bf16[1,1440,2880]{2,1,0:T(8,128)(2,1)} %param.23, f32[16,32]{1,0:T(8,128)S(1)} %select_reduce_fusion, s32[16,64]{1,0:T(8,128)S(1)} %broadcast_add_fusion, pred[16,64]{1,0:T(8,128)(4,1)S(1)} %reduce_or.9), kind=kOutput, calls=%fused_computation.9 | convolution fusion | flops 4441440256 | bytes 15674368 | tf_op jit(solution)/shard_map/nst,nsd->ntd/dot_general | solution.py:135
  143.5 0.0 reduce-scatter.5.cloned.1.call-update
  143.5 0.0 copy-start.1
  143.5 0.0 reduce-scatter.7.cloned.1.call-start
  143.6 81.9 %reduce-scatter.5.cloned.1.call-done = bf16[64,2880]{1,0:T(8,128)(2,1)} async-done(((bf16[1024,2880]{1,0:T(8,128)(2,1)}), bf16[64,2880]{1,0:T(8,128)(2,1)}) %reduce-scatter.5.cloned.1.call-update) | async-done | bytes 368656 | tf_op jit(solution)/shard_map/reduce_scatter | solution.py:144
  225.5 2.1 copy.26
  227.7 0.0 reduce-scatter.7.cloned.1.call-update
  227.7 16.4 %reduce-scatter.7.cloned.1.call-done = bf16[1440,64]{1,0:T(8,128)(2,1)} async-done(((bf16[2880,64]{1,0:T(8,128)(2,1)}), bf16[1440,64]{1,0:T(8,128)(2,1)}) %reduce-scatter.7.cloned.1.call-update) | async-done | bytes 184336
  244.0 1.1 copy.27
  245.2 0.8 add_convert_fusion.1
  246.0 0.0 copy-done.1
  (12 shorter events, 0.1 us)
Async XLA Ops:
  6.5 7.0 %copy-start = (bf16[64,512]{1,0:T(8,128)(2,1)S(1)}, bf16[64,512]{1,0:T(8,128)(2,1)}, u32[]{:S(2)}) copy-start(bf16[64,512]{1,0:T(8,128)(2,1)} %param.15) | copy-start | bytes 196612
  6.5 105.8 %all-gather.6.cloned.1.call-start = ((), (), s32[]{:S(2)}) async-start(), calls=%async_computation.3 | async-start | bytes 6406144 | tf_op jit(solution)/shard_map/all_gather | solution.py:123
  6.5 18.7 %collective-permute-start.3 = (s32[64]{0:T(128)}, s32[64]{0:T(128)S(1)}, u32[]{:S(2)}, u32[]{:S(2)}) collective-permute-start(s32[64]{0:T(128)} %param.16), channel_id=1, source_target_pairs={{0,1},{1,2},{2,3},{3,4},{4,5},{5,6},{6,7},{7,8},{8,9},{9,10},{10,1... | collective-permute-start | bytes 776 | tf_op jit(solution)/shard_map/ppermute | solution.py:18
  9.1 19.6 %collective-permute-start.2 = (s32[64]{0:T(128)}, s32[64]{0:T(128)S(1)}, u32[]{:S(2)}, u32[]{:S(2)}) collective-permute-start(s32[64]{0:T(128)} %param.16), channel_id=1, source_target_pairs={{0,2},{1,3},{2,4},{3,5},{4,6},{5,7},{6,8},{7,9},{8,10},{9,11},{10,... | collective-permute-start | bytes 776 | tf_op jit(solution)/shard_map/ppermute | solution.py:18
  13.5 16.6 %collective-permute-start.1 = (bf16[64,256]{1,0:T(8,128)(2,1)S(1)}, bf16[64,256]{1,0:T(8,128)(2,1)S(1)}, u32[]{:S(2)}, u32[]{:S(2)}) collective-permute-start(bf16[64,256]{1,0:T(8,128)(2,1)S(1)} %constant_dynamic-slice_fusion.1), channel_id=1, source_target_pairs={{0,1},{1,2},{2,3},{3,4},{4,5},{5,6},{6,7},{7,8},{8,9},{9,10},{10,1... | collective-permute-start | bytes 98312 | tf_op jit(solution)/shard_map/ppermute | solution.py:18
  16.8 13.4 %collective-permute-start = (bf16[64,256]{1,0:T(8,128)(2,1)S(1)}, bf16[64,256]{1,0:T(8,128)(2,1)S(1)}, u32[]{:S(2)}, u32[]{:S(2)}) collective-permute-start(bf16[64,256]{1,0:T(8,128)(2,1)S(1)} %constant_dynamic-slice_fusion.1), channel_id=1, source_target_pairs={{0,2},{1,3},{2,4},{3,5},{4,6},{5,7},{6,8},{7,9},{8,10},{9,11},{10,... | collective-permute-start | bytes 98312 | tf_op jit(solution)/shard_map/ppermute | solution.py:18
  21.0 9.3 %collective-permute-start.5 = (bf16[64,256]{1,0:T(8,128)(2,1)S(1)}, bf16[64,256]{1,0:T(8,128)(2,1)S(1)}, u32[]{:S(2)}, u32[]{:S(2)}) collective-permute-start(bf16[64,256]{1,0:T(8,128)(2,1)S(1)} %constant_dynamic-slice_fusion), channel_id=1, source_target_pairs={{0,1},{1,2},{2,3},{3,4},{4,5},{5,6},{6,7},{7,8},{8,9},{9,10},{10,1... | collective-permute-start | bytes 98312 | tf_op jit(solution)/shard_map/ppermute | solution.py:18
  25.2 5.1 %collective-permute-start.4 = (bf16[64,256]{1,0:T(8,128)(2,1)S(1)}, bf16[64,256]{1,0:T(8,128)(2,1)S(1)}, u32[]{:S(2)}, u32[]{:S(2)}) collective-permute-start(bf16[64,256]{1,0:T(8,128)(2,1)S(1)} %constant_dynamic-slice_fusion), channel_id=1, source_target_pairs={{0,2},{1,3},{2,4},{3,5},{4,6},{5,7},{6,8},{7,9},{8,10},{9,11},{10,... | collective-permute-start | bytes 98312 | tf_op jit(solution)/shard_map/ppermute | solution.py:18
  30.5 4.4 %copy-start.2 = (bf16[2048,2880]{0,1:T(8,128)(2,1)S(1)}, bf16[2048,2880]{0,1:T(8,128)(2,1)}, u32[]{:S(2)}) copy-start(bf16[2048,2880]{0,1:T(8,128)(2,1)} %param.18) | copy-start | bytes 35389444
  34.8 16.0 %copy-start.3 = (bf16[64,2880]{1,0:T(8,128)(2,1)S(1)}, bf16[64,2880]{1,0:T(8,128)(2,1)}, u32[]{:S(2)}) copy-start(bf16[64,2880]{1,0:T(8,128)(2,1)} %param.12) | copy-start | bytes 1105924
  38.5 12.6 %copy-start.4 = (f32[2880]{0:T(1024)S(1)}, f32[2880]{0:T(1024)}, u32[]{:S(2)}) copy-start(f32[2880]{0:T(1024)} %param.19) | copy-start | bytes 34564
  38.5 13.6 %copy-start.5 = (s32[64,4]{0,1:T(4,128)S(1)}, s32[64,4]{0,1:T(4,128)}, u32[]{:S(2)}) copy-start(s32[64,4]{0,1:T(4,128)} %param.20) | copy-start | bytes 3076
  38.5 13.6 %copy-start.6 = (f32[64,4]{0,1:T(4,128)S(1)}, f32[64,4]{0,1:T(4,128)}, u32[]{:S(2)}) copy-start(f32[64,4]{0,1:T(4,128)} %param.21) | copy-start | bytes 3076
  52.1 173.5 %reduce-scatter.5.cloned.1.call-start = ((), (), s32[]{:S(2)}) async-start(), calls=%async_computation.2 | async-start | bytes 6406144 | tf_op jit(solution)/shard_map/reduce_scatter | solution.py:144
  143.5 102.5 %copy-start.1 = (bf16[64,512]{1,0:T(8,128)(2,1)S(1)}, bf16[64,512]{1,0:T(8,128)(2,1)}, u32[]{:S(2)}) copy-start(bf16[64,512]{1,0:T(8,128)(2,1)} %param.15) | copy-start | bytes 196612
  143.5 100.5 %reduce-scatter.7.cloned.1.call-start = ((), (), s32[]{:S(2)}) async-start(), calls=%async_computation.4 | async-start | bytes 1105920
Sparse Core Ops, SparseCore 0:
  52.2 60.0 all-gather.5
  143.7 81.8 reduce-scatter.4
  227.8 16.1 reduce-scatter.6
